TPU v7x, 128 devices: a whole 4x4x4 slice. The times are simulated.
128 devices in a mesh: group: 16 (over x, z), local: 8 (over y, core).
Axes of the slice: x: 4, y: 4, z: 4, core: 2. Of those that a mesh axis runs over, the one named last changes fastest.
Arguments:
- ids: int32 [16384, 128, 8], P(('group', 'local')), may hold values from 0 to 4095
- lengths: int32 [16384, 128], P(('group', 'local')), may hold values from 1 to 8, as said below
- id_weights: float32 [16384, 128, 8], P(('group', 'local')), may hold values from 0.5 to 1.5
- table: float32 [524288, 256], P(('group', 'local')), may hold values from -2.4 to 2.4
Outputs:
- pooled: float32 [16384, 128, 256], P(('group', 'local'))
Inputs may be any that keep to these rules, and one draw needn't show every extreme that they name: `lengths`: every draw has some bag with 8 live ids.
All inputs are finite; a program needn't handle non-finite values.
Results may differ from a plain program's by a relative error of at most 0.00002.
Values sent between devices are 32-bit elements; how exact they have to be, the bound alone decides.
A program may use at most 128 MiB of HBM per device.

v0:
```python
import jax
import jax.numpy as jnp
from jax import lax
from jax.sharding import PartitionSpec as P


def cut_along(value, dim, peers):
    before, after = (value.shape[:dim], value.shape[dim + 1 :])
    return jnp.moveaxis(value.reshape(*before, peers, -1, *after), dim, 0)


def piece_ends(length, count):
    unit = 8 if length >= 8 * count else 1
    return [length // unit * k // count * unit for k in range(1, count)]


def in_order(parts, dim):
    dims = list(parts.shape[1:])
    dims[dim] *= parts.shape[0]
    return jnp.moveaxis(parts, 0, dim).reshape(dims)


def exchange_in_pieces(value, axis, pieces, split_dim, concat_dim):
    parts = cut_along(value, split_dim, lax.axis_size(axis))
    widest = max(range(1, max(2, parts.ndim - 1)), key=lambda d: parts.shape[d])
    finished = []
    for share in jnp.split(parts, piece_ends(parts.shape[widest], pieces), axis=widest):
        if share.size:
            finished.append(lax.all_to_all(share, axis, split_axis=0, concat_axis=0, tiled=True))
    return in_order(jnp.concatenate(finished, axis=widest), concat_dim)


def pool_block(table, pair):
    rows = jnp.take(table, pair[0], axis=0)
    return jnp.sum(rows * pair[1][:, :, None], axis=1)


def partial_pool(table):

    def apply_block(pair):
        return pool_block(table, pair)

    return apply_block


def body(ids, lengths, id_weights, table):
    examples, tables, bag = ids.shape
    n_group = lax.axis_size("group")
    n_local = lax.axis_size("local")
    devices = n_group * n_local
    tab_dev = tables // devices
    rows_each = table.shape[0] // tab_dev
    width = table.shape[1]
    slot = lax.broadcasted_iota(jnp.int32, ids.shape, 2)
    masked = jnp.where(slot < lengths[:, :, None], id_weights, jnp.zeros_like(id_weights))
    packed = jnp.concatenate([ids.astype(jnp.float32), masked], axis=2)
    arrived = lax.all_to_all(packed, ("group", "local"), split_axis=1, concat_axis=0, tiled=True)
    offsets = (jnp.arange(tab_dev, dtype=jnp.int32) * rows_each)[None, :, None]
    index = arrived[:, :, :bag].astype(jnp.int32) + offsets
    weights = arrived[:, :, bag:]
    per_step = max(1, 512 // (examples * tab_dev))
    while devices % per_step:
        per_step = per_step // 2
    blocks = devices // per_step
    block_rows = per_step * examples * tab_dev
    pooled = lax.map(
        partial_pool(table),
        (index.reshape(blocks, block_rows, bag), weights.reshape(blocks, block_rows, bag)),
    )
    pooled = pooled.reshape(devices * examples, tab_dev, width)
    result = exchange_in_pieces(pooled, ("group", "local"), 2, 0, 1)
    return result


def solution(mesh):
    placed = (
        P(("group", "local"), None, None),
        P(("group", "local"), None),
        P(("group", "local"), None, None),
        P(("group", "local"), None),
    )
    return jax.shard_map(
        body,
        mesh=mesh,
        in_specs=placed,
        out_specs=P(("group", "local"), None, None),
        check_vma=False,
    )
```

profile of v0, /device:TPU:1, one launch (start us, length us, event | category | flops | bytes accessed | tf_op | source)
XLA Modules:
  0.0 1149.2 jit_solution(4938456642195393215)
XLA Ops:
  4.7 11.5 %all-to-all-start = ((f32[128,128,16]{0,2,1:T(8,128)}), f32[128,128,16]{0,2,1:T(8,128)S(1)}, u32[]{:S(2)}, u32[]{:S(2)}) async-start(f32[128,128,16]{0,2,1:T(8,128)} %pad_maximum_fusion), calls=%async_computation | async-start | bytes 2097152 | tf_op jit(solution)/shard_map/all_to_all | solution.py:57
  16.2 19.1 %all-to-all-done = f32[128,128,16]{0,2,1:T(8,128)S(1)} async-done(((f32[128,128,16]{0,2,1:T(8,128)}), f32[128,128,16]{0,2,1:T(8,128)S(1)}, u32[]{:S(2)}, u32[]{:S(2)}) %all-to-all-start) | async-done | bytes 1048608 | tf_op jit(solution)/shard_map/all_to_all | solution.py:57
  45.2 867.1 %while.10 = (s32[]{:T(128)}, f32[32,512,256]{2,1,0:T(8,128)}, s32[32,512,8]{2,1,0:T(8,128)}, f32[4096,256]{1,0:T(8,128)}, f32[32,512,8]{2,1,0:T(8,128)}, /*index=5*/s32[]{:T(128)}) while((s32[]{:T(128)}, f32[32,512,256]{2,1,0:T(8,128)}, s32[32,512,8]{2,1,0:T(8,128)}, f32[4096,256]{1,0:T(8,128)}, f32[32,512,8]{2,1,0:T(8,128)}, ...), condition=%wide.region_2.3_spmd, body=%wide.region_0.2_spmd.sunk | while | flops 3055618 | bytes 14344785 | solution.py:66
  46.3 18.4 %gather_fusion = f32[4096,256]{1,0:T(8,128)} fusion(f32[4096,256]{1,0:T(8,128)} %get-tuple-element.103, s32[4096]{0:T(1024)S(1)} %broadcast_clamp_fusion.2), kind=kCustom, calls=%fused_computation.clone.1 | custom fusion | bytes 8404992 | tf_op jit(solution)/shard_map/while/body/eval_jaxpr/jit(_take)/gather | solution.py:34
  66.7 4.7 fusion.5
  73.4 18.4 %gather_fusion = f32[4096,256]{1,0:T(8,128)} fusion(f32[4096,256]{1,0:T(8,128)} %get-tuple-element.103, s32[4096]{0:T(1024)S(1)} %broadcast_clamp_fusion.2), kind=kCustom, calls=%fused_computation.clone.1 | custom fusion | bytes 8404992 | tf_op jit(solution)/shard_map/while/body/eval_jaxpr/jit(_take)/gather | solution.py:34
  93.8 4.7 fusion.5
  100.5 18.4 %gather_fusion = f32[4096,256]{1,0:T(8,128)} fusion(f32[4096,256]{1,0:T(8,128)} %get-tuple-element.103, s32[4096]{0:T(1024)S(1)} %broadcast_clamp_fusion.2), kind=kCustom, calls=%fused_computation.clone.1 | custom fusion | bytes 8404992 | tf_op jit(solution)/shard_map/while/body/eval_jaxpr/jit(_take)/gather | solution.py:34
  120.9 4.7 fusion.5
  127.6 18.4 %gather_fusion = f32[4096,256]{1,0:T(8,128)} fusion(f32[4096,256]{1,0:T(8,128)} %get-tuple-element.103, s32[4096]{0:T(1024)S(1)} %broadcast_clamp_fusion.2), kind=kCustom, calls=%fused_computation.clone.1 | custom fusion | bytes 8404992 | tf_op jit(solution)/shard_map/while/body/eval_jaxpr/jit(_take)/gather | solution.py:34
  148.0 4.7 fusion.5
  154.7 18.4 %gather_fusion = f32[4096,256]{1,0:T(8,128)} fusion(f32[4096,256]{1,0:T(8,128)} %get-tuple-element.103, s32[4096]{0:T(1024)S(1)} %broadcast_clamp_fusion.2), kind=kCustom, calls=%fused_computation.clone.1 | custom fusion | bytes 8404992 | tf_op jit(solution)/shard_map/while/body/eval_jaxpr/jit(_take)/gather | solution.py:34
  175.1 4.7 fusion.5
  181.8 18.4 %gather_fusion = f32[4096,256]{1,0:T(8,128)} fusion(f32[4096,256]{1,0:T(8,128)} %get-tuple-element.103, s32[4096]{0:T(1024)S(1)} %broadcast_clamp_fusion.2), kind=kCustom, calls=%fused_computation.clone.1 | custom fusion | bytes 8404992 | tf_op jit(solution)/shard_map/while/body/eval_jaxpr/jit(_take)/gather | solution.py:34
  202.2 4.7 fusion.5
  208.9 18.4 %gather_fusion = f32[4096,256]{1,0:T(8,128)} fusion(f32[4096,256]{1,0:T(8,128)} %get-tuple-element.103, s32[4096]{0:T(1024)S(1)} %broadcast_clamp_fusion.2), kind=kCustom, calls=%fused_computation.clone.1 | custom fusion | bytes 8404992 | tf_op jit(solution)/shard_map/while/body/eval_jaxpr/jit(_take)/gather | solution.py:34
  229.3 4.7 fusion.5
  236.0 18.4 %gather_fusion = f32[4096,256]{1,0:T(8,128)} fusion(f32[4096,256]{1,0:T(8,128)} %get-tuple-element.103, s32[4096]{0:T(1024)S(1)} %broadcast_clamp_fusion.2), kind=kCustom, calls=%fused_computation.clone.1 | custom fusion | bytes 8404992 | tf_op jit(solution)/shard_map/while/body/eval_jaxpr/jit(_take)/gather | solution.py:34
  256.4 4.7 fusion.5
  263.1 18.4 %gather_fusion = f32[4096,256]{1,0:T(8,128)} fusion(f32[4096,256]{1,0:T(8,128)} %get-tuple-element.103, s32[4096]{0:T(1024)S(1)} %broadcast_clamp_fusion.2), kind=kCustom, calls=%fused_computation.clone.1 | custom fusion | bytes 8404992 | tf_op jit(solution)/shard_map/while/body/eval_jaxpr/jit(_take)/gather | solution.py:34
  283.5 4.7 fusion.5
  290.2 18.4 %gather_fusion = f32[4096,256]{1,0:T(8,128)} fusion(f32[4096,256]{1,0:T(8,128)} %get-tuple-element.103, s32[4096]{0:T(1024)S(1)} %broadcast_clamp_fusion.2), kind=kCustom, calls=%fused_computation.clone.1 | custom fusion | bytes 8404992 | tf_op jit(solution)/shard_map/while/body/eval_jaxpr/jit(_take)/gather | solution.py:34
  310.6 4.7 fusion.5
  317.3 18.4 %gather_fusion = f32[4096,256]{1,0:T(8,128)} fusion(f32[4096,256]{1,0:T(8,128)} %get-tuple-element.103, s32[4096]{0:T(1024)S(1)} %broadcast_clamp_fusion.2), kind=kCustom, calls=%fused_computation.clone.1 | custom fusion | bytes 8404992 | tf_op jit(solution)/shard_map/while/body/eval_jaxpr/jit(_take)/gather | solution.py:34
  337.7 4.7 fusion.5
  344.4 18.4 %gather_fusion = f32[4096,256]{1,0:T(8,128)} fusion(f32[4096,256]{1,0:T(8,128)} %get-tuple-element.103, s32[4096]{0:T(1024)S(1)} %broadcast_clamp_fusion.2), kind=kCustom, calls=%fused_computation.clone.1 | custom fusion | bytes 8404992 | tf_op jit(solution)/shard_map/while/body/eval_jaxpr/jit(_take)/gather | solution.py:34
  364.8 4.7 fusion.5
  371.5 18.4 %gather_fusion = f32[4096,256]{1,0:T(8,128)} fusion(f32[4096,256]{1,0:T(8,128)} %get-tuple-element.103, s32[4096]{0:T(1024)S(1)} %broadcast_clamp_fusion.2), kind=kCustom, calls=%fused_computation.clone.1 | custom fusion | bytes 8404992 | tf_op jit(solution)/shard_map/while/body/eval_jaxpr/jit(_take)/gather | solution.py:34
  391.9 4.7 fusion.5
  398.6 18.4 %gather_fusion = f32[4096,256]{1,0:T(8,128)} fusion(f32[4096,256]{1,0:T(8,128)} %get-tuple-element.103, s32[4096]{0:T(1024)S(1)} %broadcast_clamp_fusion.2), kind=kCustom, calls=%fused_computation.clone.1 | custom fusion | bytes 8404992 | tf_op jit(solution)/shard_map/while/body/eval_jaxpr/jit(_take)/gather | solution.py:34
  419.0 4.7 fusion.5
  425.7 18.4 %gather_fusion = f32[4096,256]{1,0:T(8,128)} fusion(f32[4096,256]{1,0:T(8,128)} %get-tuple-element.103, s32[4096]{0:T(1024)S(1)} %broadcast_clamp_fusion.2), kind=kCustom, calls=%fused_computation.clone.1 | custom fusion | bytes 8404992 | tf_op jit(solution)/shard_map/while/body/eval_jaxpr/jit(_take)/gather | solution.py:34
  446.1 4.7 fusion.5
  452.8 18.4 %gather_fusion = f32[4096,256]{1,0:T(8,128)} fusion(f32[4096,256]{1,0:T(8,128)} %get-tuple-element.103, s32[4096]{0:T(1024)S(1)} %broadcast_clamp_fusion.2), kind=kCustom, calls=%fused_computation.clone.1 | custom fusion | bytes 8404992 | tf_op jit(solution)/shard_map/while/body/eval_jaxpr/jit(_take)/gather | solution.py:34
  473.2 4.7 fusion.5
  479.9 18.4 %gather_fusion = f32[4096,256]{1,0:T(8,128)} fusion(f32[4096,256]{1,0:T(8,128)} %get-tuple-element.103, s32[4096]{0:T(1024)S(1)} %broadcast_clamp_fusion.2), kind=kCustom, calls=%fused_computation.clone.1 | custom fusion | bytes 8404992 | tf_op jit(solution)/shard_map/while/body/eval_jaxpr/jit(_take)/gather | solution.py:34
  500.3 4.7 fusion.5
  507.0 18.4 %gather_fusion = f32[4096,256]{1,0:T(8,128)} fusion(f32[4096,256]{1,0:T(8,128)} %get-tuple-element.103, s32[4096]{0:T(1024)S(1)} %broadcast_clamp_fusion.2), kind=kCustom, calls=%fused_computation.clone.1 | custom fusion | bytes 8404992 | tf_op jit(solution)/shard_map/while/body/eval_jaxpr/jit(_take)/gather | solution.py:34
  527.4 4.7 fusion.5
  534.1 18.4 %gather_fusion = f32[4096,256]{1,0:T(8,128)} fusion(f32[4096,256]{1,0:T(8,128)} %get-tuple-element.103, s32[4096]{0:T(1024)S(1)} %broadcast_clamp_fusion.2), kind=kCustom, calls=%fused_computation.clone.1 | custom fusion | bytes 8404992 | tf_op jit(solution)/shard_map/while/body/eval_jaxpr/jit(_take)/gather | solution.py:34
  554.5 4.7 fusion.5
  561.2 18.4 %gather_fusion = f32[4096,256]{1,0:T(8,128)} fusion(f32[4096,256]{1,0:T(8,128)} %get-tuple-element.103, s32[4096]{0:T(1024)S(1)} %broadcast_clamp_fusion.2), kind=kCustom, calls=%fused_computation.clone.1 | custom fusion | bytes 8404992 | tf_op jit(solution)/shard_map/while/body/eval_jaxpr/jit(_take)/gather | solution.py:34
  581.6 4.7 fusion.5
  588.3 18.4 %gather_fusion = f32[4096,256]{1,0:T(8,128)} fusion(f32[4096,256]{1,0:T(8,128)} %get-tuple-element.103, s32[4096]{0:T(1024)S(1)} %broadcast_clamp_fusion.2), kind=kCustom, calls=%fused_computation.clone.1 | custom fusion | bytes 8404992 | tf_op jit(solution)/shard_map/while/body/eval_jaxpr/jit(_take)/gather | solution.py:34
  608.6 4.7 fusion.5
  615.4 18.4 %gather_fusion = f32[4096,256]{1,0:T(8,128)} fusion(f32[4096,256]{1,0:T(8,128)} %get-tuple-element.103, s32[4096]{0:T(1024)S(1)} %broadcast_clamp_fusion.2), kind=kCustom, calls=%fused_computation.clone.1 | custom fusion | bytes 8404992 | tf_op jit(solution)/shard_map/while/body/eval_jaxpr/jit(_take)/gather | solution.py:34
  642.5 18.4 %gather_fusion = f32[4096,256]{1,0:T(8,128)} fusion(f32[4096,256]{1,0:T(8,128)} %get-tuple-element.103, s32[4096]{0:T(1024)S(1)} %broadcast_clamp_fusion.2), kind=kCustom, calls=%fused_computation.clone.1 | custom fusion | bytes 8404992 | tf_op jit(solution)/shard_map/while/body/eval_jaxpr/jit(_take)/gather | solution.py:34
  669.6 18.4 %gather_fusion = f32[4096,256]{1,0:T(8,128)} fusion(f32[4096,256]{1,0:T(8,128)} %get-tuple-element.103, s32[4096]{0:T(1024)S(1)} %broadcast_clamp_fusion.2), kind=kCustom, calls=%fused_computation.clone.1 | custom fusion | bytes 8404992 | tf_op jit(solution)/shard_map/while/body/eval_jaxpr/jit(_take)/gather | solution.py:34
  696.7 18.4 %gather_fusion = f32[4096,256]{1,0:T(8,128)} fusion(f32[4096,256]{1,0:T(8,128)} %get-tuple-element.103, s32[4096]{0:T(1024)S(1)} %broadcast_clamp_fusion.2), kind=kCustom, calls=%fused_computation.clone.1 | custom fusion | bytes 8404992 | tf_op jit(solution)/shard_map/while/body/eval_jaxpr/jit(_take)/gather | solution.py:34
  723.8 18.4 %gather_fusion = f32[4096,256]{1,0:T(8,128)} fusion(f32[4096,256]{1,0:T(8,128)} %get-tuple-element.103, s32[4096]{0:T(1024)S(1)} %broadcast_clamp_fusion.2), kind=kCustom, calls=%fused_computation.clone.1 | custom fusion | bytes 8404992 | tf_op jit(solution)/shard_map/while/body/eval_jaxpr/jit(_take)/gather | solution.py:34
  750.9 18.4 %gather_fusion = f32[4096,256]{1,0:T(8,128)} fusion(f32[4096,256]{1,0:T(8,128)} %get-tuple-element.103, s32[4096]{0:T(1024)S(1)} %broadcast_clamp_fusion.2), kind=kCustom, calls=%fused_computation.clone.1 | custom fusion | bytes 8404992 | tf_op jit(solution)/shard_map/while/body/eval_jaxpr/jit(_take)/gather | solution.py:34
  778.0 18.4 %gather_fusion = f32[4096,256]{1,0:T(8,128)} fusion(f32[4096,256]{1,0:T(8,128)} %get-tuple-element.103, s32[4096]{0:T(1024)S(1)} %broadcast_clamp_fusion.2), kind=kCustom, calls=%fused_computation.clone.1 | custom fusion | bytes 8404992 | tf_op jit(solution)/shard_map/while/body/eval_jaxpr/jit(_take)/gather | solution.py:34
  805.1 18.4 %gather_fusion = f32[4096,256]{1,0:T(8,128)} fusion(f32[4096,256]{1,0:T(8,128)} %get-tuple-element.103, s32[4096]{0:T(1024)S(1)} %broadcast_clamp_fusion.2), kind=kCustom, calls=%fused_computation.clone.1 | custom fusion | bytes 8404992 | tf_op jit(solution)/shard_map/while/body/eval_jaxpr/jit(_take)/gather | solution.py:34
  825.4 4.7 fusion.5
  832.2 18.4 %gather_fusion = f32[4096,256]{1,0:T(8,128)} fusion(f32[4096,256]{1,0:T(8,128)} %get-tuple-element.103, s32[4096]{0:T(1024)S(1)} %broadcast_clamp_fusion.2), kind=kCustom, calls=%fused_computation.clone.1 | custom fusion | bytes 8404992 | tf_op jit(solution)/shard_map/while/body/eval_jaxpr/jit(_take)/gather | solution.py:34
  852.5 4.7 fusion.5
  859.3 18.4 %gather_fusion = f32[4096,256]{1,0:T(8,128)} fusion(f32[4096,256]{1,0:T(8,128)} %get-tuple-element.103, s32[4096]{0:T(1024)S(1)} %broadcast_clamp_fusion.2), kind=kCustom, calls=%fused_computation.clone.1 | custom fusion | bytes 8404992 | tf_op jit(solution)/shard_map/while/body/eval_jaxpr/jit(_take)/gather | solution.py:34
  879.6 4.7 fusion.5
  886.4 18.4 %gather_fusion = f32[4096,256]{1,0:T(8,128)} fusion(f32[4096,256]{1,0:T(8,128)} %get-tuple-element.103, s32[4096]{0:T(1024)S(1)} %broadcast_clamp_fusion.2), kind=kCustom, calls=%fused_computation.clone.1 | custom fusion | bytes 8404992 | tf_op jit(solution)/shard_map/while/body/eval_jaxpr/jit(_take)/gather | solution.py:34
  906.7 4.7 fusion.5
  912.3 6.5 slice_bitcast_fusion.1
  918.8 102.9 %all_to_all.28 = f32[128,64,1,256]{3,1,2,0:T(8,128)S(1)} all-to-all(f32[128,64,1,256]{3,1,2,0:T(8,128)S(1)} %get-tuple-element.53), channel_id=1, replica_groups=mesh['group'=16,'local'=8] {'group','local'}, dimensions={0} | all-to-all | bytes 16777216 | tf_op jit(solution)/shard_map/all_to_all | solution.py:29
  1021.8 105.9 %all_to_all.29 = f32[128,64,1,256]{3,1,2,0:T(8,128)S(1)} all-to-all(f32[128,64,1,256]{3,1,2,0:T(8,128)S(1)} %get-tuple-element.54), channel_id=1, replica_groups=mesh['group'=16,'local'=8] {'group','local'}, dimensions={0} | all-to-all | bytes 16777216 | tf_op jit(solution)/shard_map/all_to_all | solution.py:29
  1129.5 19.6 %copy.19 = f32[128,128,256]{2,1,0:T(8,128)} copy(f32[128,128,256]{2,0,1:T(8,128)S(1)} %maximum_bitcast_fusion) | data formatting | bytes 33554432 | tf_op jit(solution)/shard_map/reshape | solution.py:20
  (211 shorter events, 176.6 us)
Async XLA Ops:
  4.7 30.6 %all-to-all-start = ((f32[128,128,16]{0,2,1:T(8,128)}), f32[128,128,16]{0,2,1:T(8,128)S(1)}, u32[]{:S(2)}, u32[]{:S(2)}) async-start(f32[128,128,16]{0,2,1:T(8,128)} %pad_maximum_fusion), calls=%async_computation | async-start | bytes 2097152 | tf_op jit(solution)/shard_map/all_to_all | solution.py:57
where the time goes:
time: 1160 us; the launch traced here: 1150 us
  local copies, waits for them, and re-layouts  689 us (59%)
  other arithmetic  220 us (19%)
  blocking collectives  209 us (18%)
  waiting for transfers between devices  19.1 us (2%)
    gather x32, local copies, waits for them, and re-layouts, pool_block(): rows = jnp.take(table, pair[0], axis=0)  587 us
    all_to_all x2, blocking collectives, exchange_in_pieces(): lax.all_to_all(share, axis, split_axis=0, concat_axis=0, tiled=True)  209 us
    reduce_sum x32, other arithmetic, pool_block(): return jnp.sum(rows * pair[1][:, :, None], axis=1)  152 us
    and x32, other arithmetic, pool_block(): rows = jnp.take(table, pair[0], axis=0)  32.9 us
    select_n x32, other arithmetic, pool_block(): rows = jnp.take(table, pair[0], axis=0)  31.3 us
    mul x32, local copies, waits for them, and re-layouts, pool_block(): return jnp.sum(rows * pair[1][:, :, None], axis=1)  31.2 us
    dynamic_update_slice x32, local copies, waits for them, and re-layouts, body(): lax.map(partial_pool(table), (index.reshape(blocks, block_rows, bag), wei...  26.7 us
  transfers between devices with their start and end apart: 1, of which 1 were waited for; matrix products, arithmetic and copies ran while one was open for 0% of the time, Pallas kernels for 0%

commit v1 on v0

v1 whole, which is shorter than its diff:
```python
import functools

import jax
import jax.numpy as jnp
from jax import lax
from jax.experimental import pallas as pl
from jax.experimental.pallas import tpu as pltpu
from jax.sharding import PartitionSpec as P

MESH = pl.DeviceIdType.MESH
ANY = pl.BlockSpec(memory_space=pl.ANY)
SPEC = P(("group", "local"))


def pool_send_kernel(bags, ids_hbm, w_hbm, table_hbm, out_hbm, table, obuf, wbuf, ids, in_sem, id_sem, send_sem, recv_sem, own_sem):
    g, l = lax.axis_index("group"), lax.axis_index("local")
    me = g * 8 + l
    peers = ids_hbm.shape[0]
    chunks = ids_hbm.shape[1]
    lanes = ids_hbm.shape[2]
    bag = lanes // bags
    rows = 2 * bags

    table_copy = pltpu.make_async_copy(table_hbm, table, in_sem.at[0])
    w_copy = pltpu.make_async_copy(w_hbm, wbuf, in_sem.at[1])
    table_copy.start()
    w_copy.start()

    def ids_copy(ch):
        return pltpu.make_async_copy(ids_hbm.at[:, ch, :], ids.at[ch % 2], id_sem.at[ch % 2])

    ids_copy(0).start()

    barrier = pltpu.get_barrier_semaphore()

    def greet(k, _):
        d = (me + k) % peers
        pl.semaphore_signal(barrier, inc=1, device_id=(d // 8, d % 8), device_id_type=MESH)
        return 0

    lax.fori_loop(1, peers, greet, 0)
    pl.semaphore_wait(barrier, peers - 1)
    table_copy.wait()
    w_copy.wait()

    def target(k):
        q = (k * 37) % peers
        x = (g // 4 + q // 32) % 4
        z = (g % 4 + (q // 8) % 4) % 4
        y = (l // 2 + (q // 2) % 4) % 4
        c = (l % 2 + q % 2) % 2
        return x * 4 + z, y * 2 + c

    def pool(ch, d):
        slot = ch % 2
        w = jnp.broadcast_to(wbuf[d, pl.ds(ch, 1), :], (2, lanes))
        for e in range(bags):
            total = None
            for j in range(bag):
                q = e * bag + j
                row = table[pl.ds(ids[slot, d, q], 2), :]
                term = row * jnp.broadcast_to(w[:, q : q + 1], (2, lanes))
                total = term if total is None else total + term
            obuf[d, ch, pl.ds(2 * e, 2), :] = total

    def do_chunk(ch, _):
        ids_copy(ch).wait()

        @pl.when(ch + 1 < chunks)
        def _():
            ids_copy(ch + 1).start()

        def do_peer(k, _):
            tg, tl = target(k)
            d = tg * 8 + tl
            pool(ch, d)
            pltpu.make_async_remote_copy(
                obuf.at[d, ch], out_hbm.at[me, ch], send_sem, recv_sem, device_id=(tg, tl), device_id_type=MESH
            ).start()
            return 0

        lax.fori_loop(1, peers, do_peer, 0)
        pool(ch, me)
        return 0

    lax.fori_loop(0, chunks, do_chunk, 0)
    own = pltpu.make_async_copy(obuf.at[me], out_hbm.at[me], own_sem)
    own.start()
    own.wait()
    got = out_hbm.at[pl.ds(0, peers - 1)]
    pltpu.make_async_copy(got, got, send_sem).wait()
    pltpu.make_async_copy(got, got, recv_sem).wait()


def body(ids, lengths, id_weights, table):
    examples, tables, bag = ids.shape
    bags = 128 // bag
    chunks = examples // bags
    rows = table.shape[0]
    slot = lax.broadcasted_iota(jnp.int32, ids.shape, 2)
    masked = jnp.where(slot < lengths[:, :, None], id_weights, jnp.zeros_like(id_weights))

    def by_table(v):
        return jnp.transpose(v, (1, 0, 2)).reshape(tables, 1, chunks, 128)

    packed = jnp.concatenate([by_table(ids.astype(jnp.float32)), by_table(masked)], axis=1)
    arrived = lax.all_to_all(packed, ("group", "local"), split_axis=0, concat_axis=0, tiled=True)
    index = arrived[:, 0].astype(jnp.int32) * 2
    weights = arrived[:, 1]
    flat = table.reshape(rows * 2, 128)
    got = pl.pallas_call(
        functools.partial(pool_send_kernel, bags),
        out_shape=jax.ShapeDtypeStruct((tables, chunks, 2 * bags, 128), jnp.float32),
        in_specs=[ANY, ANY, ANY],
        out_specs=ANY,
        scratch_shapes=[
            pltpu.VMEM((rows * 2, 128), jnp.float32),
            pltpu.VMEM((tables, chunks, 2 * bags, 128), jnp.float32),
            pltpu.VMEM((tables, chunks, 128), jnp.float32),
            pltpu.SMEM((2, tables, 128), jnp.int32),
            pltpu.SemaphoreType.DMA((2,)),
            pltpu.SemaphoreType.DMA((2,)),
            pltpu.SemaphoreType.DMA,
            pltpu.SemaphoreType.DMA,
            pltpu.SemaphoreType.DMA,
        ],
        compiler_params=pltpu.CompilerParams(vmem_limit_bytes=40 << 20, collective_id=0, has_side_effects=True),
        name="pool_send",
    )(index, weights, flat)
    return jnp.transpose(got.reshape(tables, examples, 256), (1, 0, 2))


def solution(mesh):
    return jax.shard_map(body, mesh=mesh, in_specs=(SPEC,) * 4, out_specs=SPEC, check_vma=False)
```

time: 1160 us -> 410 us (0.35)
  local copies, waits for them, and re-layouts: 689 us -> 45.2 us
  Pallas kernels: 0 us -> 336 us
  other arithmetic: 220 us -> 2.31 us
  blocking collectives: 209 us -> 0 us
    gather x32 -> x0, local copies, waits for them, and re-layouts: 587 us -> none  [pool_block(): rows = jnp.take(table, pair[0], axis=0)]
    pallas_call x0 -> x1, Pallas kernels: none -> 336 us  [body(): pl.pallas_call(functools.partial(pool_send_kernel, bags), out_shape=jax.S...]
    all_to_all x2 -> x0, blocking collectives: 209 us -> none  [exchange_in_pieces(): lax.all_to_all(share, axis, split_axis=0, concat_axis=0, tiled=True)]
    reduce_sum x32 -> x0, other arithmetic: 152 us -> none  [pool_block(): return jnp.sum(rows * pair[1][:, :, None], axis=1)]
    and x32 -> x0, other arithmetic: 32.9 us -> none  [pool_block(): rows = jnp.take(table, pair[0], axis=0)]
    select_n x32 -> x0, other arithmetic: 31.3 us -> none  [pool_block(): rows = jnp.take(table, pair[0], axis=0)]
    mul x32 -> x0, local copies, waits for them, and re-layouts: 31.2 us -> none  [pool_block(): return jnp.sum(rows * pair[1][:, :, None], axis=1)]
    dynamic_update_slice x32 -> x0, local copies, waits for them, and re-layouts: 26.7 us -> none  [body(): lax.map(partial_pool(table), (index.reshape(blocks, block_rows, bag), wei...]
  transfers between devices with their start and end apart: 1 -> 1, of which waited for: 1 -> 1; matrix products, arithmetic and copies ran while one was open for 0% -> 1% of each run, Pallas kernels for 0% -> 0%
where the time goes in v1:
time: 410 us; the launch traced here: 409 us
  Pallas kernels  336 us (82%)
  local copies, waits for them, and re-layouts  45.2 us (11%)
  waiting for transfers between devices  14.3 us (3%)
  starting transfers between devices  11.5 us (3%)
    pallas_call x1, Pallas kernels, body(): pl.pallas_call(functools.partial(pool_send_kernel, bags), out_shape=jax.S...  336 us
    reshape x2, local copies, waits for them, and re-layouts, body(): return jnp.transpose(got.reshape(tables, examples, 256), (1, 0, 2))  36.9 us
    all_to_all x1, waiting for transfers between devices, body(): lax.all_to_all(packed, ('group', 'local'), split_axis=0, concat_axis=0, t...  14.3 us
    all_to_all x1, starting transfers between devices, body(): lax.all_to_all(packed, ('group', 'local'), split_axis=0, concat_axis=0, t...  11.5 us
  transfers between devices with their start and end apart: 1, of which 1 were waited for; matrix products, arithmetic and copies ran while one was open for 1% of the time, Pallas kernels for 0%

profile of v1, /device:TPU:1, one launch (start us, length us, event | category | flops | bytes accessed | tf_op | source)
XLA Modules:
  0.0 409.5 jit_solution(9903250814606466819)
XLA Ops:
  0.0 1.1 convert_element_type.7
  1.1 1.1 fusion.3
  2.2 0.1 pad_maximum_fusion
  2.3 1.4 copy.11
  3.6 11.5 %all-to-all-start = ((f32[128,2,8,128]{3,2,1,0:T(8,128)}), f32[128,2,8,128]{3,2,1,0:T(8,128)S(1)}, u32[]{:S(2)}, u32[]{:S(2)}) async-start(f32[128,2,8,128]{3,2,1,0:T(8,128)} %copy.11), calls=%async_computation | async-start | bytes 2097152 | tf_op jit(solution)/shard_map/all_to_all | solution.py:107
  15.2 4.7 %reshape.18.table_hbm = f32[8192,128]{1,0:T(8,128)} reshape(f32[4096,256]{1,0:T(8,128)} %param.7) | data formatting | bytes 8388608 | tf_op jit(solution)/shard_map/reshape | solution.py:110
  19.9 14.3 %all-to-all-done = f32[128,2,8,128]{3,2,1,0:T(8,128)S(1)} async-done(((f32[128,2,8,128]{3,2,1,0:T(8,128)}), f32[128,2,8,128]{3,2,1,0:T(8,128)S(1)}, u32[]{:S(2)}, u32[]{:S(2)}) %all-to-all-start) | async-done | bytes 1048608 | tf_op jit(solution)/shard_map/all_to_all | solution.py:107
  34.2 0.1 fusion.2.ids_hbm
  34.3 0.0 copy-start
  34.3 2.2 copy-done
  36.5 336.1 %pool_send.1 = f32[128,8,32,128]{3,2,1,0:T(8,128)} custom-call(s32[128,8,128]{2,1,0:T(8,128)S(1)} %fusion.2.ids_hbm, f32[128,8,128]{2,1,0:T(8,128)S(1)} %slice_bitcast_fusion.w_hbm, f32[8192,128]{1,0:T(8,128)S(1)} %copy-done), custom_call_target="tpu_custom_call" | custom-call | tf_op jit(solution)/shard_map/pool_send/pallas_call | solution.py:111
  372.6 19.1 %reshape.19 = f32[128,128,256]{2,1,0:T(8,128)} reshape(f32[128,8,32,128]{3,2,1,0:T(8,128)} %pool_send.1) | data formatting | bytes 33554432 | tf_op jit(solution)/shard_map/reshape | solution.py:130
  391.7 17.8 %copy.18 = f32[128,128,256]{2,0,1:T(8,128)} copy(f32[128,128,256]{2,1,0:T(8,128)} %reshape.19) | data formatting | bytes 33554432 | tf_op jit(solution)/shard_map/reshape | solution.py:130
  (1 shorter events, 0.0 us)
Async XLA Ops:
  3.6 30.6 %all-to-all-start = ((f32[128,2,8,128]{3,2,1,0:T(8,128)}), f32[128,2,8,128]{3,2,1,0:T(8,128)S(1)}, u32[]{:S(2)}, u32[]{:S(2)}) async-start(f32[128,2,8,128]{3,2,1,0:T(8,128)} %copy.11), calls=%async_computation | async-start | bytes 2097152 | tf_op jit(solution)/shard_map/all_to_all | solution.py:107
  34.3 2.2 copy-start

commit v2 on v1

v2 whole, which is shorter than its diff:
```python
import functools

import jax
import jax.numpy as jnp
from jax import lax
from jax.experimental import pallas as pl
from jax.experimental.pallas import tpu as pltpu
from jax.sharding import PartitionSpec as P

MESH = pl.DeviceIdType.MESH
ANY = pl.BlockSpec(memory_space=pl.ANY)
SPEC = P(("group", "local"))
LANES = 128
BAG = 8
BAGS = 16
PAD = 8


def pool_send_kernel(ids_hbm, w_hbm, table_hbm, out_hbm, table, obuf, ids_v, wbuf, ids, in_sem, id_sem, send_sem, recv_sem, own_sem):
    g, l = lax.axis_index("group"), lax.axis_index("local")
    me = g * 8 + l
    peers = out_hbm.shape[0]
    pieces = out_hbm.shape[1]
    groups = peers // 8
    steps = pieces * groups

    rows = table_hbm.shape[0]
    table_copy = pltpu.make_async_copy(table_hbm, table.at[pl.ds(PAD, rows)], in_sem.at[0])
    w_copy = pltpu.make_async_copy(w_hbm, wbuf, in_sem.at[1])
    i_copy = pltpu.make_async_copy(ids_hbm, ids_v, in_sem.at[2])
    i_copy.start()
    table_copy.start()
    w_copy.start()
    table[pl.ds(0, PAD), :] = jnp.zeros((PAD, LANES), jnp.float32)
    table[pl.ds(PAD + rows, PAD), :] = jnp.zeros((PAD, LANES), jnp.float32)

    barrier = pltpu.get_barrier_semaphore()

    def greet(k, _):
        d = lax.rem(me + k, peers)
        pl.semaphore_signal(barrier, inc=1, device_id=(lax.div(d, 8), lax.rem(d, 8)), device_id_type=MESH)
        return 0

    lax.fori_loop(1, peers, greet, 0)
    i_copy.wait()

    gx, gz = lax.div(g, 4), lax.rem(g, 4)

    def piece_group(i):
        ch = lax.div(i, groups)
        q = lax.rem(i * 5 + ch * 3, groups)
        return ch, lax.rem(gx + lax.div(q, 4), 4) * 4 + lax.rem(gz + lax.rem(q, 4), 4)

    def ids_copy(i, slot):
        ch, tg = piece_group(i)
        return pltpu.make_async_copy(ids_v.at[ch, pl.ds(tg * 8, 8)], ids.at[slot], id_sem.at[slot])

    ids_copy(0, 0).start()
    ids_copy(1, 1).start()
    pl.semaphore_wait(barrier, peers - 1)
    table_copy.wait()
    w_copy.wait()

    quarter = lax.broadcasted_iota(jnp.int32, (8, LANES), 0) // 2

    def pool(slot, tl, d, ch):
        shift = lax.rem(128 - lax.rem(ch, 4) * 32, 128)
        w = pltpu.roll(wbuf[d, lax.div(ch, 4)], shift, 1)
        for quad in range(BAGS // 4):
            total = None
            for j in range(BAG):
                row = None
                for a in range(4):
                    one = table[pl.ds(ids[slot, tl, (quad * 4 + a) * BAG + j], 8), :]
                    row = one if a == 0 else jnp.where(quarter == a, one, row)
                q = quad * BAG + j
                term = row * jnp.broadcast_to(w[:, q : q + 1], (8, LANES))
                total = term if total is None else total + term
            obuf[d, ch, pl.ds(8 * quad, 8), :] = total

    def step(t, _):
        for slot in range(2):
            i = t * 2 + slot
            ch, tg = piece_group(i)
            ids_copy(i, slot).wait()
            for tl in range(8):
                d = tg * 8 + tl
                pool(slot, tl, d, ch)

                @pl.when(d != me)
                def _():
                    pltpu.make_async_remote_copy(
                        obuf.at[d, ch], out_hbm.at[me, ch], send_sem, recv_sem, device_id=(tg, tl), device_id_type=MESH
                    ).start()

            @pl.when(i + 2 < steps)
            def _():
                ids_copy(i + 2, slot).start()

        return 0

    lax.fori_loop(0, steps // 2, step, 0)
    own = pltpu.make_async_copy(obuf.at[me], out_hbm.at[me], own_sem)
    own.start()
    own.wait()
    got = out_hbm.at[pl.ds(0, peers - 1)]
    pltpu.make_async_copy(got, got, send_sem).wait()
    pltpu.make_async_copy(got, got, recv_sem).wait()


def body(ids, lengths, id_weights, table):
    examples, tables, bag = ids.shape
    pieces = examples // BAGS
    rows = table.shape[0]
    slot = lax.broadcasted_iota(jnp.int32, ids.shape, 2)
    masked = jnp.where(slot < lengths[:, :, None], id_weights, jnp.zeros_like(id_weights))

    def by_table(v):
        return jnp.transpose(v, (1, 0, 2)).reshape(tables, 1, pieces, LANES)

    packed = jnp.concatenate([by_table(ids.astype(jnp.float32)), by_table(masked)], axis=1)
    arrived = lax.all_to_all(packed, ("group", "local"), split_axis=0, concat_axis=0, tiled=True)
    place = lax.broadcasted_iota(jnp.int32, (1, 1, LANES), 2) // BAG % 4
    index = jnp.transpose(arrived[:, 0].astype(jnp.int32), (1, 0, 2)) * 2 + (PAD - 2 * place)
    weights = arrived[:, 1].reshape(tables, 2, 4, 4, 4, BAG)
    weights = jnp.transpose(weights, (0, 1, 4, 2, 3, 5)).reshape(tables, 2, 4, 1, LANES)
    weights = jnp.broadcast_to(weights, (tables, 2, 4, 2, LANES)).reshape(tables, 2, 8, LANES)
    flat = table.reshape(rows * 2, LANES)
    got = pl.pallas_call(
        pool_send_kernel,
        out_shape=jax.ShapeDtypeStruct((tables, pieces, 2 * BAGS, LANES), jnp.float32),
        in_specs=[ANY, ANY, ANY],
        out_specs=ANY,
        scratch_shapes=[
            pltpu.VMEM((rows * 2 + 2 * PAD, LANES), jnp.float32),
            pltpu.VMEM((tables, pieces, 2 * BAGS, LANES), jnp.float32),
            pltpu.VMEM((pieces, tables, LANES), jnp.int32),
            pltpu.VMEM((tables, 2, 8, LANES), jnp.float32),
            pltpu.SMEM((2, 8, LANES), jnp.int32),
            pltpu.SemaphoreType.DMA((3,)),
            pltpu.SemaphoreType.DMA((2,)),
            pltpu.SemaphoreType.DMA,
            pltpu.SemaphoreType.DMA,
            pltpu.SemaphoreType.DMA,
        ],
        compiler_params=pltpu.CompilerParams(vmem_limit_bytes=40 << 20, collective_id=0, has_side_effects=True),
        name="pool_send",
    )(index, weights, flat)
    return jnp.transpose(got.reshape(tables, examples, 256), (1, 0, 2))


def solution(mesh):
    return jax.shard_map(body, mesh=mesh, in_specs=(SPEC,) * 4, out_specs=SPEC, check_vma=False)
```

time: 410 us -> 290 us (0.71)
  Pallas kernels: 336 us -> 213 us
    pallas_call x1, Pallas kernels: 336 us -> 213 us  [body(): pl.pallas_call(pool_send_kernel, out_shape=jax.ShapeDtypeStruct((tables,...]
  transfers between devices with their start and end apart: 1 -> 1, of which waited for: 1 -> 1; matrix products, arithmetic and copies ran while one was open for 1% -> 2% of each run, Pallas kernels for 0% -> 0%
where the time goes in v2:
time: 290 us; the launch traced here: 288 us
  Pallas kernels  213 us (73%)
  local copies, waits for them, and re-layouts  46.1 us (16%)
  waiting for transfers between devices  14.3 us (5%)
  starting transfers between devices  11.5 us (4%)
    pallas_call x1, Pallas kernels, body(): pl.pallas_call(pool_send_kernel, out_shape=jax.ShapeDtypeStruct((tables,...  213 us
    reshape x2, local copies, waits for them, and re-layouts, body(): return jnp.transpose(got.reshape(tables, examples, 256), (1, 0, 2))  36.9 us
    all_to_all x1, waiting for transfers between devices, body(): lax.all_to_all(packed, ('group', 'local'), split_axis=0, concat_axis=0, t...  14.3 us
    all_to_all x1, starting transfers between devices, body(): lax.all_to_all(packed, ('group', 'local'), split_axis=0, concat_axis=0, t...  11.5 us
  transfers between devices with their start and end apart: 1, of which 1 were waited for; matrix products, arithmetic and copies ran while one was open for 2% of the time, Pallas kernels for 0%

profile of v2, /device:TPU:1, one launch (start us, length us, event | category | flops | bytes accessed | tf_op | source)
XLA Modules:
  0.0 287.5 jit_solution(10283076898609517948)
XLA Ops:
  0.0 1.1 convert_element_type.7
  1.1 1.1 fusion.4
  2.2 0.1 pad_maximum_fusion
  2.3 1.4 copy.12
  3.6 11.5 %all-to-all-start = ((f32[128,2,8,128]{3,2,1,0:T(8,128)}), f32[128,2,8,128]{3,2,1,0:T(8,128)S(1)}, u32[]{:S(2)}, u32[]{:S(2)}) async-start(f32[128,2,8,128]{3,2,1,0:T(8,128)} %copy.12), calls=%async_computation | async-start | bytes 2097152 | tf_op jit(solution)/shard_map/all_to_all | solution.py:122
  15.1 4.7 %reshape.82.table_hbm = f32[8192,128]{1,0:T(8,128)} reshape(f32[4096,256]{1,0:T(8,128)} %param.7) | data formatting | bytes 8388608 | tf_op jit(solution)/shard_map/reshape | solution.py:128
  19.9 14.3 %all-to-all-done = f32[128,2,8,128]{3,2,1,0:T(8,128)S(1)} async-done(((f32[128,2,8,128]{3,2,1,0:T(8,128)}), f32[128,2,8,128]{3,2,1,0:T(8,128)S(1)}, u32[]{:S(2)}, u32[]{:S(2)}) %all-to-all-start) | async-done | bytes 1048608 | tf_op jit(solution)/shard_map/all_to_all | solution.py:122
  34.2 0.1 fusion.8
  34.3 0.2 copy.19
  34.5 0.1 copy.15
  34.6 0.3 copy.16
  34.9 0.1 fusion.3.ids_hbm
  35.0 0.4 broadcast_in_dim.13
  35.4 0.0 copy-start
  35.4 2.2 copy-done
  37.5 213.1 %pool_send.1 = f32[128,8,32,128]{3,2,1,0:T(8,128)} custom-call(s32[8,128,128]{2,1,0:T(8,128)S(1)} %fusion.3.ids_hbm, f32[128,2,8,128]{3,2,1,0:T(8,128)S(1)} %bitcast.24, f32[8192,128]{1,0:T(8,128)S(1)} %copy-done), custom_call_target="tpu_custom_call" | custom-call | tf_op jit(solution)/shard_map/pool_send/pallas_call | solution.py:129
  250.7 19.1 %reshape.83 = f32[128,128,256]{2,1,0:T(8,128)} reshape(f32[128,8,32,128]{3,2,1,0:T(8,128)} %pool_send.1) | data formatting | bytes 33554432 | tf_op jit(solution)/shard_map/reshape | solution.py:149
  269.7 17.8 %copy.30 = f32[128,128,256]{2,0,1:T(8,128)} copy(f32[128,128,256]{2,1,0:T(8,128)} %reshape.83) | data formatting | bytes 33554432 | tf_op jit(solution)/shard_map/reshape | solution.py:149
  (1 shorter events, 0.0 us)
Async XLA Ops:
  3.6 30.6 %all-to-all-start = ((f32[128,2,8,128]{3,2,1,0:T(8,128)}), f32[128,2,8,128]{3,2,1,0:T(8,128)S(1)}, u32[]{:S(2)}, u32[]{:S(2)}) async-start(f32[128,2,8,128]{3,2,1,0:T(8,128)} %copy.12), calls=%async_computation | async-start | bytes 2097152 | tf_op jit(solution)/shard_map/all_to_all | solution.py:122
  35.4 2.2 copy-start

commit v3 on v2

v3 whole, which is shorter than its diff:
```python
import jax
import jax.numpy as jnp
from jax import lax
from jax.experimental import pallas as pl
from jax.experimental.pallas import tpu as pltpu
from jax.sharding import PartitionSpec as P

MESH = pl.DeviceIdType.MESH
ANY = pl.BlockSpec(memory_space=pl.ANY)
HBM = pl.BlockSpec(memory_space=pltpu.HBM)
VMEM = pl.BlockSpec(memory_space=pltpu.VMEM)
SPEC = P(("group", "local"))
LANES = 128
BAG = 8
BAGS = 16
PAD = 8


def pool_send_kernel(
    ids_in, w_in, table_hbm, got, raw, table, obuf, ids_v, w_v, ids, raw_sem, stage_sem, ask_sem, ids_sem, w_sem, send_sem, recv_sem
):
    g, l = lax.axis_index("group"), lax.axis_index("local")
    me = g * 8 + l
    pieces, peers = got.shape[0], got.shape[2]
    groups = peers // 8
    steps = pieces * groups
    rows = table_hbm.shape[0]

    raw_copy = pltpu.make_async_copy(table_hbm, raw, raw_sem)
    raw_copy.start()

    barrier = pltpu.get_barrier_semaphore()

    def greet(k, _):
        d = lax.rem(me + k, peers)
        pl.semaphore_signal(barrier, inc=1, device_id=(lax.div(d, 8), lax.rem(d, 8)), device_id_type=MESH)
        return 0

    lax.fori_loop(1, peers, greet, 0)

    gx, gz = lax.div(g, 4), lax.rem(g, 4)
    pltpu.make_async_copy(ids_in.at[me], ids_v.at[me], ids_sem.at[g]).start()
    pltpu.make_async_copy(w_in.at[me], w_v.at[me], w_sem.at[g]).start()
    pl.semaphore_wait(barrier, peers - 1)

    def ask(i, _):
        q = lax.rem(i * 5, groups)
        tg = lax.rem(gx + 4 - lax.div(q, 4), 4) * 4 + lax.rem(gz + 4 - lax.rem(q, 4), 4)
        for tl in range(8):
            d = tg * 8 + tl

            @pl.when(d != me)
            def _():
                to = dict(device_id=(tg, tl), device_id_type=MESH)
                pltpu.make_async_remote_copy(ids_in.at[d], ids_v.at[me], ask_sem, ids_sem.at[g], **to).start()
                pltpu.make_async_remote_copy(w_in.at[d], w_v.at[me], ask_sem, w_sem.at[g], **to).start()

        return 0

    lax.fori_loop(0, groups, ask, 0)

    table[pl.ds(0, PAD), :] = jnp.zeros((PAD, LANES), jnp.float32)
    table[pl.ds(PAD + 2 * rows, PAD), :] = jnp.zeros((PAD, LANES), jnp.float32)
    raw_copy.wait()

    def lay(t, _):
        for u in range(8):
            r = pl.multiple_of((t * 8 + u) * 8, 8)
            for h in range(2):
                table[pl.ds(PAD + 2 * r + h, 8, stride=2), :] = raw[pl.ds(r, 8), pl.ds(h * LANES, LANES)]
        return 0

    lax.fori_loop(0, rows // 64, lay, 0)

    def piece_group(i):
        ch = lax.div(i, groups)
        q = lax.rem(i * 5 + ch * 3, groups)
        return ch, lax.rem(gx + lax.div(q, 4), 4) * 4 + lax.rem(gz + lax.rem(q, 4), 4)

    def stage(i, slot):
        ch, tg = piece_group(i)
        return pltpu.make_async_copy(ids_v.at[pl.ds(tg * 8, 8), ch], ids.at[slot], stage_sem.at[slot])

    def stage_next(i, slot):
        @pl.when(i < groups)
        def _():
            _, tg = piece_group(i)
            block = ids_v.at[pl.ds(tg * 8, 8)]
            pltpu.make_async_copy(block, block, ids_sem.at[tg]).wait()
            block = w_v.at[pl.ds(tg * 8, 8)]
            pltpu.make_async_copy(block, block, w_sem.at[tg]).wait()

        stage(i, slot).start()

    stage_next(0, 0)
    stage_next(1, 1)

    quarter = lax.broadcasted_iota(jnp.int32, (8, LANES), 0) // 2

    def by_quarter(parts):
        row = parts[0]
        for a in range(1, 4):
            row = jnp.where(quarter == a, parts[a], row)
        return row

    def pool(slot, tl, d, ch):
        shift = lax.rem(128 - lax.rem(ch, 4) * 32, 128)
        half = lax.div(ch, 4) * 4
        w = by_quarter([jnp.broadcast_to(w_v[d, pl.ds(half + a, 1), :], (8, LANES)) for a in range(4)])
        w = pltpu.roll(w, shift, 1)
        for quad in range(BAGS // 4):
            total = None
            for j in range(BAG):
                row = by_quarter([table[pl.ds(ids[slot, tl, (quad * 4 + a) * BAG + j], 8), :] for a in range(4)])
                q = quad * BAG + j
                term = row * jnp.broadcast_to(w[:, q : q + 1], (8, LANES))
                total = term if total is None else total + term
            obuf[d, ch, pl.ds(8 * quad, 8), :] = total

    def step(t, _):
        for slot in range(2):
            i = t * 2 + slot
            ch, tg = piece_group(i)
            stage(i, slot).wait()
            for tl in range(8):
                d = tg * 8 + tl
                pool(slot, tl, d, ch)

                @pl.when(d != me)
                def _():
                    pltpu.make_async_remote_copy(
                        obuf.at[d, ch], got.at[ch, :, me], send_sem, recv_sem, device_id=(tg, tl), device_id_type=MESH
                    ).start()

            @pl.when(i + 2 < steps)
            def _():
                stage_next(i + 2, slot)

        return 0

    lax.fori_loop(0, steps // 2, step, 0)
    pltpu.make_async_copy(obuf.at[me], got.at[:, :, me], recv_sem).start()
    sent = obuf.at[pl.ds(0, peers - 1)]
    pltpu.make_async_copy(sent, sent, send_sem).wait()
    asked = ids_v.at[pl.ds(0, peers - 1)]
    pltpu.make_async_copy(asked, asked, ask_sem).wait()
    pltpu.make_async_copy(asked, asked, ask_sem).wait()
    pltpu.make_async_copy(got, got, recv_sem).wait()


def place_kernel(got, out_hbm, sem):
    examples = out_hbm.shape[0]
    parts = sem.shape[0]
    batch = examples // parts

    def copy(p, h):
        cut = pl.ds(p * batch, batch)
        return pltpu.make_async_copy(got.at[cut, h], out_hbm.at[cut, :, pl.ds(h * LANES, LANES)], sem.at[p, h])

    for p in range(parts):
        for h in range(2):
            copy(p, h).start()
    for p in range(parts):
        for h in range(2):
            copy(p, h).wait()


def body(ids, lengths, id_weights, table):
    examples, tables, bag = ids.shape
    pieces = examples // BAGS
    rows, width = table.shape
    slot = lax.broadcasted_iota(jnp.int32, ids.shape, 2)
    masked = jnp.where(slot < lengths[:, :, None], id_weights, jnp.zeros_like(id_weights))

    place = lax.broadcasted_iota(jnp.int32, (1, 1, LANES), 2) // BAG % 4
    index = jnp.transpose(ids, (1, 0, 2)).reshape(tables, pieces, LANES) * 2 + (PAD - 2 * place)
    weights = masked.reshape(2, 4, 4, 4, tables, bag)
    weights = jnp.transpose(weights, (4, 0, 3, 1, 2, 5)).reshape(tables, 8, LANES)
    got = pl.pallas_call(
        pool_send_kernel,
        out_shape=pltpu.VMEM((pieces, 2 * BAGS, tables, LANES), jnp.float32),
        in_specs=[ANY, ANY, HBM],
        out_specs=VMEM,
        scratch_shapes=[
            pltpu.VMEM((rows, width), jnp.float32),
            pltpu.VMEM((rows * 2 + 2 * PAD, LANES), jnp.float32),
            pltpu.VMEM((tables, pieces, 2 * BAGS, LANES), jnp.float32),
            pltpu.VMEM((tables, pieces, LANES), jnp.int32),
            pltpu.VMEM((tables, 8, LANES), jnp.float32),
            pltpu.SMEM((2, 8, LANES), jnp.int32),
            pltpu.SemaphoreType.DMA,
            pltpu.SemaphoreType.DMA((2,)),
            pltpu.SemaphoreType.DMA,
            pltpu.SemaphoreType.DMA((tables // 8,)),
            pltpu.SemaphoreType.DMA((tables // 8,)),
            pltpu.SemaphoreType.DMA,
            pltpu.SemaphoreType.DMA,
        ],
        compiler_params=pltpu.CompilerParams(vmem_limit_bytes=44 << 20, collective_id=0, has_side_effects=True),
        name="pool_send",
    )(index, weights, table)
    return pl.pallas_call(
        place_kernel,
        out_shape=jax.ShapeDtypeStruct((examples, tables, width), jnp.float32),
        in_specs=[VMEM],
        out_specs=ANY,
        scratch_shapes=[pltpu.SemaphoreType.DMA((8, 2))],
        compiler_params=pltpu.CompilerParams(vmem_limit_bytes=20 << 20),
        name="place",
    )(got.reshape(examples, 2, tables, LANES))


def solution(mesh):
    return jax.shard_map(body, mesh=mesh, in_specs=(SPEC,) * 4, out_specs=SPEC, check_vma=False)
```

time: 290 us -> 255 us (0.88)
  local copies, waits for them, and re-layouts: 46.1 us -> 1.28 us
  Pallas kernels: 213 us -> 250 us
  waiting for transfers between devices: 14.3 us -> 0 us
  starting transfers between devices: 11.5 us -> 0 us
    reshape x3 -> x1, local copies, waits for them, and re-layouts: 41.6 us -> 1 us  [body(): jnp.transpose(weights, (4, 0, 3, 1, 2, 5)).reshape(tables, 8, LANES)]
    pallas_call x1 -> x2, Pallas kernels: 213 us -> 250 us  [the longest x1 244 us: body(): pl.pallas_call(pool_send_kernel, out_shape=pltpu.VMEM((pieces, 2 * BAGS,...]
    all_to_all x1 -> x0, waiting for transfers between devices: 14.3 us -> none  [body(): lax.all_to_all(packed, ('group', 'local'), split_axis=0, concat_axis=0, t...]
    all_to_all x1 -> x0, starting transfers between devices: 11.5 us -> none  [body(): lax.all_to_all(packed, ('group', 'local'), split_axis=0, concat_axis=0, t...]
  transfers between devices with their start and end apart: 1 -> 0, of which waited for: 1 -> 0; matrix products, arithmetic and copies ran while one was open for 2% -> 0% of each run, Pallas kernels for 0% -> 0%
where the time goes in v3:
time: 255 us; the launch traced here: 254 us
  Pallas kernels  250 us (98%)
  other arithmetic  3.02 us (1%)
    pallas_call x1, Pallas kernels, body(): pl.pallas_call(pool_send_kernel, out_shape=pltpu.VMEM((pieces, 2 * BAGS,...  244 us
    pallas_call x1, Pallas kernels, body(): pl.pallas_call(place_kernel, out_shape=jax.ShapeDtypeStruct((examples, ta...  5.96 us

profile of v3, /device:TPU:1, one launch (start us, length us, event | category | flops | bytes accessed | tf_op | source)
XLA Modules:
  0.0 254.2 jit_solution(2620941824296978677)
XLA Ops:
  0.0 1.1 broadcast_multiply_fusion
  1.1 0.2 copy.9
  1.3 0.8 broadcast_add_fusion.ids_in
  2.2 1.1 fusion
  3.3 0.1 copy.10
  3.3 1.0 copy.11.w_in
  4.3 243.9 %pool_send.1 = f32[8,32,128,128]{3,2,1,0:T(8,128)S(1)} custom-call(s32[128,8,128]{2,1,0:T(8,128)} %broadcast_add_fusion.ids_in, f32[128,8,128]{2,1,0:T(8,128)} %copy.11.w_in, f32[4096,256]{1,0:T(8,128)} %table_hbm.1), custom_call_target="tpu_custom_call" | custom-call | tf_op jit(solution)/shard_map/pool_send/pallas_call | solution.py:179
  248.2 6.0 %place.1 = f32[128,128,256]{2,1,0:T(8,128)} custom-call(f32[128,2,128,128]{3,2,1,0:T(8,128)S(1)} %bitcast.8), custom_call_target="tpu_custom_call" | custom-call | tf_op jit(solution)/shard_map/place/pallas_call | solution.py:202
  (1 shorter events, 0.0 us)

commit v4 on v3

--- a/solution.py
+++ b/solution.py
@@ -13,11 +13,11 @@
 LANES = 128
 BAG = 8
 BAGS = 16
-PAD = 8
+GAP = 8
 
 
 def pool_send_kernel(
-    ids_in, w_in, table_hbm, got, raw, table, obuf, ids_v, w_v, ids, raw_sem, stage_sem, ask_sem, ids_sem, w_sem, send_sem, recv_sem
+    ids_in, w_in, table_hbm, got, table, obuf, ids_v, w_v, ids, table_sem, stage_sem, ask_sem, ids_sem, w_sem, send_sem, recv_sem
 ):
     g, l = lax.axis_index("group"), lax.axis_index("local")
     me = g * 8 + l
@@ -26,8 +26,14 @@
     steps = pieces * groups
     rows = table_hbm.shape[0]
 
-    raw_copy = pltpu.make_async_copy(table_hbm, raw, raw_sem)
-    raw_copy.start()
+    halves = [
+        pltpu.make_async_copy(
+            table_hbm.at[:, pl.ds(h * LANES, LANES)], table.at[pl.ds(h * (rows + GAP), rows)], table_sem.at[h]
+        )
+        for h in range(2)
+    ]
+    for half in halves:
+        half.start()
 
     barrier = pltpu.get_barrier_semaphore()
 
@@ -59,18 +65,8 @@
 
     lax.fori_loop(0, groups, ask, 0)
 
-    table[pl.ds(0, PAD), :] = jnp.zeros((PAD, LANES), jnp.float32)
-    table[pl.ds(PAD + 2 * rows, PAD), :] = jnp.zeros((PAD, LANES), jnp.float32)
-    raw_copy.wait()
-
-    def lay(t, _):
-        for u in range(8):
-            r = pl.multiple_of((t * 8 + u) * 8, 8)
-            for h in range(2):
-                table[pl.ds(PAD + 2 * r + h, 8, stride=2), :] = raw[pl.ds(r, 8), pl.ds(h * LANES, LANES)]
-        return 0
-
-    lax.fori_loop(0, rows // 64, lay, 0)
+    for half in halves:
+        half.wait()
 
     def piece_group(i):
         ch = lax.div(i, groups)
@@ -95,27 +91,27 @@
     stage_next(0, 0)
     stage_next(1, 1)
 
-    quarter = lax.broadcasted_iota(jnp.int32, (8, LANES), 0) // 2
-
-    def by_quarter(parts):
-        row = parts[0]
-        for a in range(1, 4):
-            row = jnp.where(quarter == a, parts[a], row)
-        return row
+    sublane = lax.broadcasted_iota(jnp.int32, (8, LANES), 0)
 
     def pool(slot, tl, d, ch):
-        shift = lax.rem(128 - lax.rem(ch, 4) * 32, 128)
-        half = lax.div(ch, 4) * 4
-        w = by_quarter([jnp.broadcast_to(w_v[d, pl.ds(half + a, 1), :], (8, LANES)) for a in range(4)])
-        w = pltpu.roll(w, shift, 1)
-        for quad in range(BAGS // 4):
-            total = None
+        w = pltpu.roll(w_v[d], lax.rem(LANES - ch * 2 * BAG, LANES), 1)
+        for octet in range(BAGS // 8):
+            totals = [None, None]
             for j in range(BAG):
-                row = by_quarter([table[pl.ds(ids[slot, tl, (quad * 4 + a) * BAG + j], 8), :] for a in range(4)])
-                q = quad * BAG + j
-                term = row * jnp.broadcast_to(w[:, q : q + 1], (8, LANES))
-                total = term if total is None else total + term
-            obuf[d, ch, pl.ds(8 * quad, 8), :] = total
+                picked = [None, None]
+                for a in range(8):
+                    r = ids[slot, tl, (octet * 8 + a) * BAG + j]
+                    for h in range(2):
+                        half = table if h == 0 else table.at[pl.ds(rows + GAP, rows)]
+                        row = half[pl.ds(r, 8, stride=0), :]
+                        picked[h] = row if a == 0 else jnp.where(sublane == a, row, picked[h])
+                q = octet * BAG + j
+                weight = jnp.broadcast_to(w[:, q : q + 1], (8, LANES))
+                for h in range(2):
+                    term = picked[h] * weight
+                    totals[h] = term if j == 0 else totals[h] + term
+            for h in range(2):
+                obuf[d, ch, pl.ds((octet * 2 + h) * 8, 8), :] = totals[h]
 
     def step(t, _):
         for slot in range(2):
@@ -149,13 +145,10 @@
 
 
 def place_kernel(got, out_hbm, sem):
-    examples = out_hbm.shape[0]
-    parts = sem.shape[0]
-    batch = examples // parts
+    parts = got.shape[0]
 
     def copy(p, h):
-        cut = pl.ds(p * batch, batch)
-        return pltpu.make_async_copy(got.at[cut, h], out_hbm.at[cut, :, pl.ds(h * LANES, LANES)], sem.at[p, h])
+        return pltpu.make_async_copy(got.at[p, h], out_hbm.at[pl.ds(p * 8, 8), :, pl.ds(h * LANES, LANES)], sem.at[p, h])
 
     for p in range(parts):
         for h in range(2):
@@ -172,23 +165,21 @@
     slot = lax.broadcasted_iota(jnp.int32, ids.shape, 2)
     masked = jnp.where(slot < lengths[:, :, None], id_weights, jnp.zeros_like(id_weights))
 
-    place = lax.broadcasted_iota(jnp.int32, (1, 1, LANES), 2) // BAG % 4
-    index = jnp.transpose(ids, (1, 0, 2)).reshape(tables, pieces, LANES) * 2 + (PAD - 2 * place)
-    weights = masked.reshape(2, 4, 4, 4, tables, bag)
-    weights = jnp.transpose(weights, (4, 0, 3, 1, 2, 5)).reshape(tables, 8, LANES)
+    index = jnp.transpose(ids, (1, 0, 2)).reshape(tables, pieces, LANES)
+    weights = masked.reshape(pieces * 2, 8, tables, bag)
+    weights = jnp.transpose(weights, (2, 1, 0, 3)).reshape(tables, 8, LANES)
     got = pl.pallas_call(
         pool_send_kernel,
         out_shape=pltpu.VMEM((pieces, 2 * BAGS, tables, LANES), jnp.float32),
         in_specs=[ANY, ANY, HBM],
         out_specs=VMEM,
         scratch_shapes=[
-            pltpu.VMEM((rows, width), jnp.float32),
-            pltpu.VMEM((rows * 2 + 2 * PAD, LANES), jnp.float32),
+            pltpu.VMEM((rows * 2 + GAP, LANES), jnp.float32),
             pltpu.VMEM((tables, pieces, 2 * BAGS, LANES), jnp.float32),
             pltpu.VMEM((tables, pieces, LANES), jnp.int32),
             pltpu.VMEM((tables, 8, LANES), jnp.float32),
             pltpu.SMEM((2, 8, LANES), jnp.int32),
-            pltpu.SemaphoreType.DMA,
+            pltpu.SemaphoreType.DMA((2,)),
             pltpu.SemaphoreType.DMA((2,)),
             pltpu.SemaphoreType.DMA,
             pltpu.SemaphoreType.DMA((tables // 8,)),
@@ -204,10 +195,10 @@
         out_shape=jax.ShapeDtypeStruct((examples, tables, width), jnp.float32),
         in_specs=[VMEM],
         out_specs=ANY,
-        scratch_shapes=[pltpu.SemaphoreType.DMA((8, 2))],
+        scratch_shapes=[pltpu.SemaphoreType.DMA((examples // 8, 2))],
         compiler_params=pltpu.CompilerParams(vmem_limit_bytes=20 << 20),
         name="place",
-    )(got.reshape(examples, 2, tables, LANES))
+    )(got.reshape(examples // 8, 2, 8, tables, LANES))
 
 
 def solution(mesh):

time: 255 us -> 229 us (0.90)
  Pallas kernels: 250 us -> 224 us
    pallas_call x1, Pallas kernels: 244 us -> 218 us  [body(): pl.pallas_call(pool_send_kernel, out_shape=pltpu.VMEM((pieces, 2 * BAGS,...]
where the time goes in v4:
time: 229 us; the launch traced here: 228 us
  Pallas kernels  224 us (98%)
  local copies, waits for them, and re-layouts  3.06 us (1%)
    pallas_call x1, Pallas kernels, body(): pl.pallas_call(pool_send_kernel, out_shape=pltpu.VMEM((pieces, 2 * BAGS,...  218 us
    pallas_call x1, Pallas kernels, body(): pl.pallas_call(place_kernel, out_shape=jax.ShapeDtypeStruct((examples, ta...  6.08 us

profile of v4, /device:TPU:1, one launch (start us, length us, event | category | flops | bytes accessed | tf_op | source)
XLA Modules:
  0.0 228.4 jit_solution(18246675547923220335)
XLA Ops:
  0.0 2.0 copy.10.ids_in
  2.0 1.1 fusion
  3.2 1.0 copy.11.w_in
  4.2 218.1 %pool_send.1 = f32[8,32,128,128]{3,2,1,0:T(8,128)S(1)} custom-call(s32[128,8,128]{2,1,0:T(8,128)} %copy.10.ids_in, f32[128,8,128]{2,1,0:T(8,128)} %copy.11.w_in, f32[4096,256]{1,0:T(8,128)} %table_hbm.1), custom_call_target="tpu_custom_call" | custom-call | tf_op jit(solution)/shard_map/pool_send/pallas_call | solution.py:171
  222.3 6.1 %place.1 = f32[128,128,256]{2,1,0:T(8,128)} custom-call(f32[16,2,8,128,128]{4,3,2,1,0:T(8,128)S(1)} %bitcast.10), custom_call_target="tpu_custom_call" | custom-call | tf_op jit(solution)/shard_map/place/pallas_call | solution.py:193
  (1 shorter events, 0.0 us)

commit v5 on v4

--- a/solution.py
+++ b/solution.py
@@ -45,21 +45,26 @@
     lax.fori_loop(1, peers, greet, 0)
 
     gx, gz = lax.div(g, 4), lax.rem(g, 4)
-    pltpu.make_async_copy(ids_in.at[me], ids_v.at[me], ids_sem.at[g]).start()
-    pltpu.make_async_copy(w_in.at[me], w_v.at[me], w_sem.at[g]).start()
+    y, c = lax.div(l, 2), lax.rem(l, 2)
+    pltpu.make_async_copy(ids_in.at[me], ids_v.at[g * 8], ids_sem.at[g]).start()
+    pltpu.make_async_copy(w_in.at[me], w_v.at[g * 8], w_sem.at[g]).start()
     pl.semaphore_wait(barrier, peers - 1)
 
     def ask(i, _):
-        q = lax.rem(i * 5, groups)
+        ch = 0
+        b = lax.rem(lax.rem(lax.div(i, 2), 8) * 5 + ch * 3, 8)
+        q = lax.rem(lax.div(b, 4) + 2 * lax.rem(i, 2), 4) * 4 + lax.rem(lax.rem(b, 4) + 2 * lax.rem(i, 2), 4)
         tg = lax.rem(gx + 4 - lax.div(q, 4), 4) * 4 + lax.rem(gz + 4 - lax.rem(q, 4), 4)
-        for tl in range(8):
+        for r in range(8):
+            tl = lax.rem(y + 4 - r // 2, 4) * 2 + lax.rem(c + r % 2, 2)
             d = tg * 8 + tl
+            row = g * 8 + r
 
             @pl.when(d != me)
             def _():
                 to = dict(device_id=(tg, tl), device_id_type=MESH)
-                pltpu.make_async_remote_copy(ids_in.at[d], ids_v.at[me], ask_sem, ids_sem.at[g], **to).start()
-                pltpu.make_async_remote_copy(w_in.at[d], w_v.at[me], ask_sem, w_sem.at[g], **to).start()
+                pltpu.make_async_remote_copy(ids_in.at[d], ids_v.at[row], ask_sem, ids_sem.at[g], **to).start()
+                pltpu.make_async_remote_copy(w_in.at[d], w_v.at[row], ask_sem, w_sem.at[g], **to).start()
 
         return 0
 
@@ -70,7 +75,8 @@
 
     def piece_group(i):
         ch = lax.div(i, groups)
-        q = lax.rem(i * 5 + ch * 3, groups)
+        b = lax.rem(lax.rem(lax.div(i, 2), 8) * 5 + ch * 3, 8)
+        q = lax.rem(lax.div(b, 4) + 2 * lax.rem(i, 2), 4) * 4 + lax.rem(lax.rem(b, 4) + 2 * lax.rem(i, 2), 4)
         return ch, lax.rem(gx + lax.div(q, 4), 4) * 4 + lax.rem(gz + lax.rem(q, 4), 4)
 
     def stage(i, slot):
@@ -93,8 +99,8 @@
 
     sublane = lax.broadcasted_iota(jnp.int32, (8, LANES), 0)
 
-    def pool(slot, tl, d, ch):
-        w = pltpu.roll(w_v[d], lax.rem(LANES - ch * 2 * BAG, LANES), 1)
+    def pool(slot, tl, row_of, d, ch):
+        w = pltpu.roll(w_v[row_of], lax.rem(LANES - ch * 2 * BAG, LANES), 1)
         for octet in range(BAGS // 8):
             totals = [None, None]
             for j in range(BAG):
@@ -118,9 +124,10 @@
             i = t * 2 + slot
             ch, tg = piece_group(i)
             stage(i, slot).wait()
-            for tl in range(8):
+            for r in (0, 3, 6, 1, 4, 7, 2, 5):
+                tl = lax.rem(y + r // 2, 4) * 2 + lax.rem(c + r % 2, 2)
                 d = tg * 8 + tl
-                pool(slot, tl, d, ch)
+                pool(slot, r, tg * 8 + r, d, ch)
 
                 @pl.when(d != me)
                 def _():

time: 229 us -> 218 us (0.952)
  Pallas kernels: 224 us -> 214 us
    pallas_call x1, Pallas kernels: 218 us -> 208 us  [body(): pl.pallas_call(pool_send_kernel, out_shape=pltpu.VMEM((pieces, 2 * BAGS,...]
where the time goes in v5:
time: 218 us
  Pallas kernels  214 us (98%)
  local copies, waits for them, and re-layouts  3.06 us (1%)
    pallas_call x1, Pallas kernels, body(): pl.pallas_call(pool_send_kernel, out_shape=pltpu.VMEM((pieces, 2 * BAGS,...  208 us
    pallas_call x1, Pallas kernels, body(): pl.pallas_call(place_kernel, out_shape=jax.ShapeDtypeStruct((examples, ta...  6.08 us

profile of v5, /device:TPU:1, one launch (start us, length us, event | category | flops | bytes accessed | tf_op | source)
XLA Modules:
  0.0 217.8 jit_solution(7425844936922284975)
XLA Ops:
  0.0 2.0 copy.10.ids_in
  2.0 1.1 fusion
  3.2 1.0 copy.11.w_in
  4.2 207.5 %pool_send.1 = f32[8,32,128,128]{3,2,1,0:T(8,128)S(1)} custom-call(s32[128,8,128]{2,1,0:T(8,128)} %copy.10.ids_in, f32[128,8,128]{2,1,0:T(8,128)} %copy.11.w_in, f32[4096,256]{1,0:T(8,128)} %table_hbm.1), custom_call_target="tpu_custom_call" | custom-call | tf_op jit(solution)/shard_map/pool_send/pallas_call | solution.py:178
  211.7 6.1 %place.1 = f32[128,128,256]{2,1,0:T(8,128)} custom-call(f32[16,2,8,128,128]{4,3,2,1,0:T(8,128)S(1)} %bitcast.10), custom_call_target="tpu_custom_call" | custom-call | tf_op jit(solution)/shard_map/place/pallas_call | solution.py:200
  (1 shorter events, 0.0 us)

commit v6 on v5

--- a/solution.py
+++ b/solution.py
@@ -17,7 +17,7 @@
 
 
 def pool_send_kernel(
-    ids_in, w_in, table_hbm, got, table, obuf, ids_v, w_v, ids, table_sem, stage_sem, ask_sem, ids_sem, w_sem, send_sem, recv_sem
+    ids_hbm, len_hbm, w_hbm, table_hbm, got, table, obuf, ids_e, len_e, w_e, ids_in, w_in, ids_v, w_v, ids, in_sem, table_sem, stage_sem, ask_sem, ids_sem, w_sem, send_sem, recv_sem
 ):
     g, l = lax.axis_index("group"), lax.axis_index("local")
     me = g * 8 + l
@@ -32,8 +32,12 @@
         )
         for h in range(2)
     ]
-    for half in halves:
-        half.start()
+    inputs = [
+        pltpu.make_async_copy(whole, here, in_sem.at[k])
+        for k, (whole, here) in enumerate(((ids_hbm, ids_e), (len_hbm, len_e.at[pl.ds(0, len_hbm.shape[0])]), (w_hbm, w_e)))
+    ]
+    for copy in inputs + halves:
+        copy.start()
 
     barrier = pltpu.get_barrier_semaphore()
 
@@ -46,8 +50,31 @@
 
     gx, gz = lax.div(g, 4), lax.rem(g, 4)
     y, c = lax.div(l, 2), lax.rem(l, 2)
-    pltpu.make_async_copy(ids_in.at[me], ids_v.at[g * 8], ids_sem.at[g]).start()
-    pltpu.make_async_copy(w_in.at[me], w_v.at[g * 8], w_sem.at[g]).start()
+    for copy in inputs:
+        copy.wait()
+
+    sublane = lax.broadcasted_iota(jnp.int32, (8, LANES), 0)
+
+    def turn(k, _):
+        by_id = ids_e[pl.ds(pl.multiple_of(k * LANES, LANES), LANES), :].T
+        live = []
+        for p in range(LANES // 8):
+            e = p * 8 + k
+            weight = w_e[pl.ds(pl.multiple_of(e * 8, 8), 8), :]
+            live.append(jnp.where(sublane < len_e[pl.ds(e, 8, stride=0), :], weight, jnp.zeros_like(weight)))
+        by_weight = jnp.concatenate(live, axis=0).T
+        for t in range(peers // 8):
+            ids_in[pl.ds(t * 64 + k, 8, stride=8), :] = by_id[t * 8 : t * 8 + 8]
+            w_in[pl.ds(t * 64 + k, 8, stride=8), :] = by_weight[t * 8 : t * 8 + 8]
+        return 0
+
+    lax.fori_loop(0, 8, turn, 0)
+
+    def tile(ref, d):
+        return ref.at[pl.ds(pl.multiple_of(d * 8, 8), 8)]
+
+    pltpu.make_async_copy(tile(ids_in, me), ids_v.at[g * 8], ids_sem.at[g]).start()
+    pltpu.make_async_copy(tile(w_in, me), w_v.at[g * 8], w_sem.at[g]).start()
     pl.semaphore_wait(barrier, peers - 1)
 
     def ask(i, _):
@@ -63,8 +90,8 @@
             @pl.when(d != me)
             def _():
                 to = dict(device_id=(tg, tl), device_id_type=MESH)
-                pltpu.make_async_remote_copy(ids_in.at[d], ids_v.at[row], ask_sem, ids_sem.at[g], **to).start()
-                pltpu.make_async_remote_copy(w_in.at[d], w_v.at[row], ask_sem, w_sem.at[g], **to).start()
+                pltpu.make_async_remote_copy(tile(ids_in, d), ids_v.at[row], ask_sem, ids_sem.at[g], **to).start()
+                pltpu.make_async_remote_copy(tile(w_in, d), w_v.at[row], ask_sem, w_sem.at[g], **to).start()
 
         return 0
 
@@ -96,8 +123,6 @@
 
     stage_next(0, 0)
     stage_next(1, 1)
-
-    sublane = lax.broadcasted_iota(jnp.int32, (8, LANES), 0)
 
     def pool(slot, tl, row_of, d, ch):
         w = pltpu.roll(w_v[row_of], lax.rem(LANES - ch * 2 * BAG, LANES), 1)
@@ -108,7 +133,7 @@
                 for a in range(8):
                     r = ids[slot, tl, (octet * 8 + a) * BAG + j]
                     for h in range(2):
-                        half = table if h == 0 else table.at[pl.ds(rows + GAP, rows)]
+                        half = table if h == 0 else table.at[pl.ds(rows + GAP, rows + 8)]
                         row = half[pl.ds(r, 8, stride=0), :]
                         picked[h] = row if a == 0 else jnp.where(sublane == a, row, picked[h])
                 q = octet * BAG + j
@@ -169,23 +194,27 @@
     examples, tables, bag = ids.shape
     pieces = examples // BAGS
     rows, width = table.shape
-    slot = lax.broadcasted_iota(jnp.int32, ids.shape, 2)
-    masked = jnp.where(slot < lengths[:, :, None], id_weights, jnp.zeros_like(id_weights))
-
-    index = jnp.transpose(ids, (1, 0, 2)).reshape(tables, pieces, LANES)
-    weights = masked.reshape(pieces * 2, 8, tables, bag)
-    weights = jnp.transpose(weights, (2, 1, 0, 3)).reshape(tables, 8, LANES)
+
+    def by_slot(v):
+        return jnp.transpose(v, (0, 2, 1)).reshape(examples * bag, tables)
+
     got = pl.pallas_call(
         pool_send_kernel,
         out_shape=pltpu.VMEM((pieces, 2 * BAGS, tables, LANES), jnp.float32),
-        in_specs=[ANY, ANY, HBM],
+        in_specs=[HBM] * 4,
         out_specs=VMEM,
         scratch_shapes=[
-            pltpu.VMEM((rows * 2 + GAP, LANES), jnp.float32),
+            pltpu.VMEM((rows * 2 + GAP + 8, LANES), jnp.float32),
             pltpu.VMEM((tables, pieces, 2 * BAGS, LANES), jnp.float32),
+            pltpu.VMEM((examples * bag, tables), jnp.int32),
+            pltpu.VMEM((examples + 8, tables), jnp.int32),
+            pltpu.VMEM((examples * bag, tables), jnp.float32),
+            pltpu.VMEM((tables * pieces, LANES), jnp.int32),
+            pltpu.VMEM((tables * 8, LANES), jnp.float32),
             pltpu.VMEM((tables, pieces, LANES), jnp.int32),
             pltpu.VMEM((tables, 8, LANES), jnp.float32),
             pltpu.SMEM((2, 8, LANES), jnp.int32),
+            pltpu.SemaphoreType.DMA((3,)),
             pltpu.SemaphoreType.DMA((2,)),
             pltpu.SemaphoreType.DMA((2,)),
             pltpu.SemaphoreType.DMA,
@@ -196,7 +225,7 @@
         ],
         compiler_params=pltpu.CompilerParams(vmem_limit_bytes=44 << 20, collective_id=0, has_side_effects=True),
         name="pool_send",
-    )(index, weights, table)
+    )(by_slot(ids), lengths, by_slot(id_weights), table)
     return pl.pallas_call(
         place_kernel,
         out_shape=jax.ShapeDtypeStruct((examples, tables, width), jnp.float32),

time: 218 us -> 214 us (0.982)
  local copies, waits for them, and re-layouts: 3.06 us -> 0 us
    reshape x2 -> x0, local copies, waits for them, and re-layouts: 3.03 us -> none  [the longest x1 2.04 us: body(): index = jnp.transpose(ids, (1, 0, 2)).reshape(tables, pieces, LANES)]
where the time goes in v6:
time: 214 us
  Pallas kernels  214 us (100%)
    pallas_call x1, Pallas kernels, body(): pl.pallas_call(pool_send_kernel, out_shape=pltpu.VMEM((pieces, 2 * BAGS,...  207 us
    pallas_call x1, Pallas kernels, body(): pl.pallas_call(place_kernel, out_shape=jax.ShapeDtypeStruct((examples, ta...  6.08 us

profile of v6, /device:TPU:1, one launch (start us, length us, event | category | flops | bytes accessed | tf_op | source)
XLA Modules:
  0.0 213.5 jit_solution(16816069034704547183)
XLA Ops:
  0.0 207.4 %pool_send.1 = f32[8,32,128,128]{3,2,1,0:T(8,128)S(1)} custom-call(s32[1024,128]{1,0:T(8,128)} %bitcast.8, s32[128,128]{1,0:T(8,128)} %len_hbm.1, f32[1024,128]{1,0:T(8,128)} %bitcast.9, f32[4096,256]{1,0:T(8,128)} %table_hbm.1), custom_call_target="tpu_custom_call" | custom-call | tf_op jit(solution)/shard_map/pool_send/pallas_call | solution.py:201
  207.4 6.1 %place.1 = f32[128,128,256]{2,1,0:T(8,128)} custom-call(f32[16,2,8,128,128]{4,3,2,1,0:T(8,128)S(1)} %bitcast.7), custom_call_target="tpu_custom_call" | custom-call | tf_op jit(solution)/shard_map/place/pallas_call | solution.py:229

commit v7 on v6

--- a/solution.py
+++ b/solution.py
@@ -42,11 +42,16 @@
     barrier = pltpu.get_barrier_semaphore()
 
     def greet(k, _):
-        d = lax.rem(me + k, peers)
-        pl.semaphore_signal(barrier, inc=1, device_id=(lax.div(d, 8), lax.rem(d, 8)), device_id_type=MESH)
-        return 0
-
-    lax.fori_loop(1, peers, greet, 0)
+        tg = lax.rem(g + k, groups)
+        for tl in range(8):
+
+            @pl.when(tg * 8 + tl != me)
+            def _():
+                pl.semaphore_signal(barrier, inc=1, device_id=(tg, tl), device_id_type=MESH)
+
+        return 0
+
+    lax.fori_loop(0, groups, greet, 0)
 
     gx, gz = lax.div(g, 4), lax.rem(g, 4)
     y, c = lax.div(l, 2), lax.rem(l, 2)
@@ -79,7 +84,7 @@
 
     def ask(i, _):
         ch = 0
-        b = lax.rem(lax.rem(lax.div(i, 2), 8) * 5 + ch * 3, 8)
+        b = lax.rem(lax.rem(lax.div(i, 2), 8) * 7 + ch * 5, 8)
         q = lax.rem(lax.div(b, 4) + 2 * lax.rem(i, 2), 4) * 4 + lax.rem(lax.rem(b, 4) + 2 * lax.rem(i, 2), 4)
         tg = lax.rem(gx + 4 - lax.div(q, 4), 4) * 4 + lax.rem(gz + 4 - lax.rem(q, 4), 4)
         for r in range(8):
@@ -102,7 +107,7 @@
 
     def piece_group(i):
         ch = lax.div(i, groups)
-        b = lax.rem(lax.rem(lax.div(i, 2), 8) * 5 + ch * 3, 8)
+        b = lax.rem(lax.rem(lax.div(i, 2), 8) * 7 + ch * 5, 8)
         q = lax.rem(lax.div(b, 4) + 2 * lax.rem(i, 2), 4) * 4 + lax.rem(lax.rem(b, 4) + 2 * lax.rem(i, 2), 4)
         return ch, lax.rem(gx + lax.div(q, 4), 4) * 4 + lax.rem(gz + lax.rem(q, 4), 4)
 

time: 214 us -> 213 us (level)
  no operation moved by 1% of the time
where the time goes in v7:
time: 213 us
  Pallas kernels  213 us (100%)
    pallas_call x1, Pallas kernels, body(): pl.pallas_call(pool_send_kernel, out_shape=pltpu.VMEM((pieces, 2 * BAGS,...  207 us
    pallas_call x1, Pallas kernels, body(): pl.pallas_call(place_kernel, out_shape=jax.ShapeDtypeStruct((examples, ta...  6.08 us

profile of v7, /device:TPU:1, one launch (start us, length us, event | category | flops | bytes accessed | tf_op | source)
XLA Modules:
  0.0 212.9 jit_solution(3078449567799028429)
XLA Ops:
  0.0 206.8 %pool_send.1 = f32[8,32,128,128]{3,2,1,0:T(8,128)S(1)} custom-call(s32[1024,128]{1,0:T(8,128)} %bitcast.8, s32[128,128]{1,0:T(8,128)} %len_hbm.1, f32[1024,128]{1,0:T(8,128)} %bitcast.9, f32[4096,256]{1,0:T(8,128)} %table_hbm.1), custom_call_target="tpu_custom_call" | custom-call | tf_op jit(solution)/shard_map/pool_send/pallas_call | solution.py:206
  206.8 6.1 %place.1 = f32[128,128,256]{2,1,0:T(8,128)} custom-call(f32[16,2,8,128,128]{4,3,2,1,0:T(8,128)S(1)} %bitcast.7), custom_call_target="tpu_custom_call" | custom-call | tf_op jit(solution)/shard_map/place/pallas_call | solution.py:234
